TPU v7x, 32 devices: a whole 2x2x4 slice. The times are simulated.
32 devices in a mesh: lat: 16 (over z, x, core), lon: 2 (over y).
Axes of the slice: x: 2, y: 2, z: 4, core: 2. Of those that a mesh axis runs over, the one named last changes fastest.
Arguments:
- elevation: float32 [16, 1024, 1024], P(None, 'lat', 'lon'), may hold values from -6 to 6
- depth: float32 [1024, 1024], P('lat', 'lon'), may hold values from 0.3 to 3
- friction: float32 [1024, 1024], P('lat', 'lon'), may hold values from 0.05 to 1
- land_mask: int32 [1024, 1024], P('lat', 'lon'), may hold values 0 or 1
- order_map: int32 [32], replicated, may hold values from 0 to 31, each once
- legendre: bfloat16 [32, 1024, 2048], P('lon', 'lat'), may hold values from -0.1875 to 0.1875
- load: float32 [2048], replicated, may hold values from 0.25 to 4
Outputs:
- elevation_new: float32 [16, 1024, 1024], P(None, 'lat', 'lon')
- sal: float32 [16, 1024, 1024], P(None, 'lat', 'lon')
- friction_new: float32 [1024, 1024], P('lat', 'lon')
Inputs may be any that keep to these rules, and one draw needn't show every extreme that they name: `order_map`: each order 0 to 31 stands in exactly one slot. `land_mask`: 1 marks sea and 0 land.
All inputs are finite; a program needn't handle non-finite values. No bound on the sum of `land_mask` on one device may be relied on, other than what follows from the above.
Results may differ from a plain program's by a relative error of at most 0.0037.
Values may be sent and summed in bfloat16 or wider, within the bound.
A program may use at most 64 MiB of HBM per device.

v0:
```python
import functools
import math

import jax
import jax.numpy as jnp
from jax import lax
from jax.experimental import pallas as pl
from jax.experimental.pallas import tpu as pltpu
from jax.sharding import PartitionSpec as P

SAMPLES = 64


FREQUENCIES = (1.0, 1.0347, 0.9582, 1.0379, 0.5018, 0.4651, 0.4986, 0.4482)
EQ_AMPS = (0.73, 0.34, 0.14, 0.09, 0.42, 0.3, 0.14, 0.06)
LAT_EDGE = 1.3614
RELAX_RATE = 0.1
BASE_FRICTION = 0.05
DRAG_COEFF = 0.5
SPEED_EPS = 0.001
STEP_TIME = 3.0
PRECISE = lax.Precision.HIGHEST


def fourier_basis(order_map, columns, lon_count):
    product = order_map[:, None] * columns[None, :] % lon_count
    angles = product.astype(jnp.float32) * (2.0 * math.pi / lon_count)
    scaling = jnp.where(
        order_map > 0, math.sqrt(2.0 / lon_count), math.sqrt(1.0 / lon_count)
    ).astype(jnp.float32)[:, None]
    harmonics = jnp.stack([jnp.cos(angles) * scaling, jnp.sin(angles) * scaling], axis=1)
    return harmonics.reshape(2 * order_map.shape[0], columns.shape[0])


def sample_table():
    sample_time = STEP_TIME * jnp.arange(SAMPLES, dtype=jnp.float32)[:, None]
    omegas = jnp.asarray(FREQUENCIES, dtype=jnp.float32)[None, :]
    phases = sample_time * omegas
    return jnp.stack([jnp.cos(phases), jnp.sin(phases)], axis=2).reshape(
        SAMPLES, 2 * len(FREQUENCIES)
    )


def sweep_kernel(
    omega_ref,
    amp_ref,
    pole_ref,
    elev_ref,
    depth_ref,
    drag_ref,
    mask_ref,
    row_halo_ref,
    col_halo_ref,
    synth_ref,
    basis_ref,
    lat_ref,
    wave_ref,
    weight_ref,
    new_ref,
    sal_ref,
    friction_ref,
    coefs,
    east_cells,
    north_cells,
):
    k = pl.program_id(0)
    channels = 2 * pl.num_programs(0)
    lat_rows, lon_cols = depth_ref.shape
    wide_rows, wide_cols = lat_rows + 8, lon_cols + 128

    def rolled(value, shift, axis):
        return pltpu.roll(value, shift % value.shape[axis], axis)

    lane = lax.broadcasted_iota(jnp.int32, (lat_rows, 128), 1)
    line = lax.broadcasted_iota(jnp.int32, (8, lon_cols), 0)

    def widened(main, field):
        right = jnp.sum(jnp.where(lane == field, col_halo_ref[0], 0.0), axis=1, keepdims=True)
        left = jnp.sum(jnp.where(lane == 64 + field, col_halo_ref[1], 0.0), axis=1, keepdims=True)
        sides = jnp.where(lane == 0, right, jnp.where(lane == 127, left, 0.0))
        below = row_halo_ref[0, pl.ds(field, 1), :]
        above = row_halo_ref[1, pl.ds(field, 1), :]
        ends = jnp.where(line == 0, below, jnp.where(line == 7, above, 0.0))
        corner = jnp.zeros((8, 128), jnp.float32)
        return jnp.concatenate(
            [
                jnp.concatenate([main, sides], axis=1),
                jnp.concatenate([ends, corner], axis=1),
            ],
            axis=0,
        )

    inverse_cos = lat_ref[:, 2:3]
    cos_face = lat_ref[:, 3:4]

    @pl.when(k == 0)
    def _():
        depth = widened(depth_ref[...] * mask_ref[...].astype(jnp.float32), channels)
        row = lax.broadcasted_iota(jnp.int32, (wide_rows, wide_cols), 0)
        depth = jnp.where(
            row == lat_rows, depth * pole_ref[0], jnp.where(row == wide_rows - 1, depth * pole_ref[1], depth)
        )
        drag = widened(drag_ref[...], channels + 1)
        for face, axis in enumerate((1, 0)):
            square = depth * rolled(depth, -1, axis)
            mean = 0.5 * (drag + rolled(drag, -1, axis))
            coefs[4 * face] = square * mean
            coefs[4 * face + 1] = square * jnp.sqrt(square)
            coefs[4 * face + 2] = mean * mean
            coefs[4 * face + 3] = square

    omega = omega_ref[k]
    kind = k // 4
    lat_shape = amp_ref[k] * jnp.where(kind == 0, lat_ref[:, 0:1], lat_ref[:, 1:2])
    surface = []
    for part in range(2):
        sal = jnp.dot(
            synth_ref[part],
            basis_ref[...],
            precision=PRECISE,
            preferred_element_type=jnp.float32,
        )
        sal_ref[part] = sal[:lat_rows, :lon_cols]
        wave = wave_ref[pl.ds(2 * kind + part, 1), :]
        surface.append(widened(elev_ref[part], 2 * k + part) - lat_shape * wave - sal)
    divergence = [None, None]
    for face, (axis, factor, cells) in enumerate(
        ((1, inverse_cos, east_cells), (0, cos_face, north_cells))
    ):
        inverse = 1.0 / (coefs[4 * face + 2] + (omega * omega) * coefs[4 * face + 3])
        real_coef = coefs[4 * face] * inverse * factor
        imag_coef = (omega * coefs[4 * face + 1]) * inverse * factor
        diff_real = rolled(surface[0], -1, axis) - surface[0]
        diff_imag = rolled(surface[1], -1, axis) - surface[1]
        fluxes = (
            imag_coef * diff_imag - real_coef * diff_real,
            -(real_coef * diff_imag + imag_coef * diff_real),
        )
        for part, flux in enumerate(fluxes):
            back = rolled(flux, 1, axis)
            change = (flux - back)[:lat_rows, :lon_cols]
            divergence[part] = change if face == 0 else divergence[part] + change
            mean = (0.5 * (flux + back))[:lat_rows, :lon_cols]
            cells[:, pl.ds(2 * k + part, 1), :] = mean.reshape(lat_rows, 1, lon_cols)
    sea_mask = mask_ref[...].astype(jnp.float32)
    inner_cos = inverse_cos[:lat_rows]
    real, imag = elev_ref[0], elev_ref[1]
    new_ref[0] = (real - RELAX_RATE * (divergence[0] * inner_cos + omega * imag)) * sea_mask
    new_ref[1] = (imag - RELAX_RATE * (divergence[1] * inner_cos - omega * real)) * sea_mask

    @pl.when(k == pl.num_programs(0) - 1)
    def _():
        weights = weight_ref[...]
        weights_top = weights.astype(jnp.bfloat16)
        weights_rest = (weights - weights_top.astype(jnp.float32)).astype(jnp.bfloat16)
        stacked = jnp.concatenate([weights_top, weights_top, weights_rest], axis=1)

        def sampled(value):
            top = value.astype(jnp.bfloat16)
            rest = (value - top.astype(jnp.float32)).astype(jnp.bfloat16)
            return jnp.dot(
                stacked,
                jnp.concatenate([top, rest, top], axis=0),
                preferred_element_type=jnp.float32,
            )

        @pl.loop(0, lat_rows)
        def _(j):
            east, north = sampled(east_cells[j]), sampled(north_cells[j])
            squares = east * east + north * north + SPEED_EPS * SPEED_EPS
            speeds = squares * lax.rsqrt(squares)
            mean = jnp.sum(speeds, axis=0, keepdims=True) * (DRAG_COEFF / SAMPLES)
            friction_ref[pl.ds(j, 1), :] = BASE_FRICTION + mean


def sweep(elevation, depth, friction, land_mask, halos, synth, basis, lat_table, waves, poles):
    channels, lat_rows, lon_cols = elevation.shape
    wide_rows, wide_cols = lat_rows + 8, lon_cols + 128
    whole = pl.BlockSpec(memory_space=pltpu.VMEM)
    scalars = pl.BlockSpec(memory_space=pltpu.SMEM)

    def pair(*shape):
        return pl.BlockSpec((2,) + shape, lambda k: (k, 0, 0))

    return pl.pallas_call(
        sweep_kernel,
        grid=(channels // 2,),
        out_shape=[
            jax.ShapeDtypeStruct(elevation.shape, jnp.float32),
            jax.ShapeDtypeStruct(elevation.shape, jnp.float32),
            jax.ShapeDtypeStruct(depth.shape, jnp.float32),
        ],
        in_specs=[scalars] * 3
        + [pair(lat_rows, lon_cols)]
        + [whole] * 5
        + [pair(wide_rows, basis.shape[0])]
        + [whole] * 4,
        out_specs=[
            pair(lat_rows, lon_cols),
            pair(lat_rows, lon_cols),
            pl.BlockSpec((lat_rows, lon_cols), lambda k: (0, 0)),
        ],
        scratch_shapes=[
            pltpu.VMEM((8, wide_rows, wide_cols), jnp.float32),
            pltpu.VMEM((lat_rows, channels, lon_cols), jnp.float32),
            pltpu.VMEM((lat_rows, channels, lon_cols), jnp.float32),
        ],
        compiler_params=pltpu.CompilerParams(
            dimension_semantics=("arbitrary",), vmem_limit_bytes=40 * 1024 * 1024
        ),
    )(
        jnp.asarray(FREQUENCIES, dtype=jnp.float32),
        jnp.asarray(EQ_AMPS, dtype=jnp.float32),
        poles,
        elevation,
        depth,
        friction,
        land_mask,
        *halos,
        synth,
        basis,
        lat_table,
        waves,
        sample_table(),
    )


GROUPS = 4
MESH = pl.DeviceIdType.MESH


def transform_kernel(
    lat_size,
    lon_size,
    groups,
    part_ref,
    leg_ref,
    load_ref,
    leg_edges_ref,
    row_edges_ref,
    col_edges_ref,
    out_ref,
    row_halo_ref,
    col_halo_ref,
    sector_parts,
    fourier,
    leg_halo,
    synth,
    synth_edges,
    acc,
    first_recv,
    rs_send,
    rs_recv,
    gathered,
    lon_send,
    lon_recv,
    out_send,
    out_recv,
    red_send,
    red_recv,
    gat_send,
    gat_recv,
    halo_send,
    halo_recv,
):
    lat_me = lax.axis_index("lat")
    lon_me = lax.axis_index("lon")
    levels = lat_size.bit_length() - 1
    slots, lat_rows, degrees = leg_ref.shape
    quantities = part_ref.shape[2]
    rows = slots * quantities
    width = degrees // groups
    bits = [(lat_me // 2**k) % 2 for k in range(levels)]
    partners = [lat_me + (1 - 2 * bits[k]) * 2**k for k in range(levels)]
    others = [lax.rem(lon_me + d, lon_size) for d in range(1, lon_size)]
    kept, sent = [0], []
    for k in range(levels):
        half = rows >> (k + 1)
        sent.append(pl.multiple_of(kept[k] + (1 - bits[k]) * half, half))
        kept.append(pl.multiple_of(kept[k] + bits[k] * half, half))

    barrier = pltpu.get_barrier_semaphore()
    for k in range(levels):
        pl.semaphore_signal(
            barrier, inc=1, device_id=(partners[k], lon_me), device_id_type=MESH
        )
    for other in others:
        pl.semaphore_signal(barrier, inc=1, device_id=(lat_me, other), device_id_type=MESH)
    above, below = lax.rem(lat_me + lat_size - 1, lat_size), lax.rem(lat_me + 1, lat_size)
    left, right = lax.rem(lon_me + lon_size - 1, lon_size), lax.rem(lon_me + 1, lon_size)
    for near in (above, below):
        pl.semaphore_signal(barrier, inc=1, device_id=(near, lon_me), device_id_type=MESH)
    pl.semaphore_wait(barrier, levels + lon_size + 1)

    pending = []

    def send(source, target, send_sem, recv_sem, device):
        copy = pltpu.make_async_remote_copy(
            src_ref=source,
            dst_ref=target,
            send_sem=send_sem,
            recv_sem=recv_sem,
            device_id=device,
            device_id_type=MESH,
        )
        copy.start()
        pending.append(copy)
        return copy

    copies = [
        send(
            part_ref.at[other],
            sector_parts.at[d],
            lon_send.at[d],
            lon_recv.at[d],
            (lat_me, other),
        )
        for d, other in enumerate(others)
    ]
    halos = [
        send(source, target, halo_send.at[n], halo_recv.at[n], device)
        for n, (source, target, device) in enumerate(
            (
                (leg_edges_ref.at[0], leg_halo.at[pl.ds(0, slots)], (above, lon_me)),
                (leg_edges_ref.at[1], leg_halo.at[pl.ds(slots, slots)], (below, lon_me)),
                (row_edges_ref.at[0], row_halo_ref.at[0], (above, lon_me)),
                (row_edges_ref.at[1], row_halo_ref.at[1], (below, lon_me)),
                (col_edges_ref, col_halo_ref.at[0], (lat_me, left)),
                (col_edges_ref, col_halo_ref.at[1], (lat_me, right)),
            )
        )
    ]
    for copy in copies:
        copy.wait_recv()
    total = part_ref[lon_me]
    for d in range(lon_size - 1):
        total = total + sector_parts[d]
    fourier[...] = total.astype(jnp.bfloat16)

    reducing = {}
    gathering = {}

    def analyse(g):
        @pl.loop(0, slots)
        def _(s):
            acc[g, pl.ds(pl.multiple_of(s * quantities, quantities), quantities), :] = jnp.dot(
                fourier[s],
                leg_ref[s, :, g * width : (g + 1) * width],
                preferred_element_type=jnp.float32,
            )

        reducing[g] = send(
            acc.at[g, pl.ds(sent[0], rows // 2), :],
            first_recv.at[g],
            red_send.at[g, 0],
            red_recv.at[g, 0],
            (partners[0], lon_me),
        )

    def offset_of(k):
        return rows // 2 - (rows >> k)

    def reduce(g, k):
        reducing[g].wait_recv()
        size = rows >> (k + 1)

        def arrived(start, count):
            if k == 0:
                return first_recv[g, pl.ds(start, count), :]
            return rs_recv[g, pl.ds(offset_of(k) + start, count), :].astype(jnp.float32)

        if k < levels - 1:
            half = size // 2
            away = pl.multiple_of((1 - bits[k + 1]) * half, half)
            home = pl.multiple_of(bits[k + 1] * half, half)
            place = pl.ds(offset_of(k + 1), half)
            rs_send[g, place, :] = (
                acc[g, pl.ds(sent[k + 1], half), :] + arrived(away, half)
            ).astype(jnp.bfloat16)
            reducing[g] = send(
                rs_send.at[g, place, :],
                rs_recv.at[g, place, :],
                red_send.at[g, k + 1],
                red_recv.at[g, k + 1],
                (partners[k + 1], lon_me),
            )
            acc[g, pl.ds(kept[k + 1 + 1], half), :] = acc[
                g, pl.ds(kept[k + 1 + 1], half), :
            ] + arrived(home, half)
        else:
            mine = pl.ds(kept[levels], size)
            scale = load_ref[:, g * width : (g + 1) * width]
            gathered[g, mine, :] = ((acc[g, mine, :] + arrived(0, size)) * scale).astype(
                jnp.bfloat16
            )
            spread(g, levels - 1)

    def spread(g, k):
        held = pl.ds(kept[k + 1], rows >> (k + 1))
        gathering[g] = send(
            gathered.at[g, held, :],
            gathered.at[g, held, :],
            gat_send.at[g, k],
            gat_recv.at[g, k],
            (partners[k], lon_me),
        )

    def synthesise(g):
        if g == 0:
            for copy in halos[:2]:
                copy.wait_recv()
        at_edges = lax.dot_general(
            gathered[g],
            leg_halo[:, g * width : (g + 1) * width],
            (((1,), (1,)), ((), ())),
            preferred_element_type=jnp.float32,
        )
        if g == 0:
            synth_edges[...] = at_edges
        else:
            synth_edges[...] = synth_edges[...] + at_edges

        @pl.loop(0, slots)
        def _(s):
            part = lax.dot_general(
                gathered[g, pl.ds(pl.multiple_of(s * quantities, quantities), quantities), :],
                leg_ref[s, :, g * width : (g + 1) * width],
                (((1,), (1,)), ((), ())),
                preferred_element_type=jnp.float32,
            )
            if g == 0:
                synth[s] = part
            else:
                synth[s] = synth[s] + part

    def gather(g, k):
        gathering[g].wait_recv()
        if k > 0:
            spread(g, k - 1)
        else:
            synthesise(g)

    for wave in range(groups + 2 * levels):
        for g in range(groups):
            stage = wave - g
            if stage == 0:
                analyse(g)
            elif 1 <= stage <= levels:
                reduce(g, stage - 1)
            elif levels < stage <= 2 * levels:
                gather(g, 2 * levels - stage)

    lanes = lax.broadcasted_iota(jnp.int32, (quantities, 2 * slots), 1)
    places = lax.broadcasted_iota(jnp.int32, (quantities, out_ref.shape[2] - lat_rows), 1)

    @pl.loop(0, slots)
    def _(s):
        edges = synth_edges[pl.ds(pl.multiple_of(s * quantities, quantities), quantities), :]
        after = jnp.sum(jnp.where(lanes == s, edges, 0.0), axis=1, keepdims=True)
        before = jnp.sum(jnp.where(lanes == slots + s, edges, 0.0), axis=1, keepdims=True)
        out_ref[lon_me * slots + s, :, :lat_rows] = synth[s]
        out_ref[lon_me * slots + s, :, lat_rows:] = jnp.where(
            places == 0, after, jnp.where(places == 7, before, 0.0)
        )

    block = out_ref.at[pl.ds(lon_me * slots, slots)]
    copies = [
        send(block, block, out_send.at[d], out_recv.at[d], (lat_me, other))
        for d, other in enumerate(others)
    ]
    for copy in copies + halos[2:]:
        copy.wait_recv()
    for copy in pending:
        copy.wait_send()


def transform(parts, legendre, load, edges, lat_size, lon_size):
    slots, lat_rows, degrees = legendre.shape
    quantities = parts.shape[2]
    rows = slots * quantities
    groups = GROUPS
    width = degrees // groups
    levels = lat_size.bit_length() - 1
    vmem = pl.BlockSpec(memory_space=pltpu.VMEM)
    dma = pltpu.SemaphoreType.DMA
    flops = 4 * rows * lat_rows * degrees
    return pl.pallas_call(
        functools.partial(transform_kernel, lat_size, lon_size, groups),
        out_shape=[
            jax.ShapeDtypeStruct((lon_size * slots, quantities, 128), jnp.float32),
            jax.ShapeDtypeStruct(edges[1].shape, jnp.float32),
            jax.ShapeDtypeStruct((2,) + edges[2].shape, jnp.float32),
        ],
        in_specs=[vmem] * 6,
        out_specs=[vmem] * 3,
        scratch_shapes=[
            pltpu.VMEM((lon_size - 1, slots, quantities, lat_rows), jnp.float32),
            pltpu.VMEM((slots, quantities, lat_rows), jnp.bfloat16),
            pltpu.VMEM((2 * slots, degrees), jnp.bfloat16),
            pltpu.VMEM((slots, quantities, lat_rows), jnp.float32),
            pltpu.VMEM((rows, 2 * slots), jnp.float32),
            pltpu.VMEM((groups, rows, width), jnp.float32),
            pltpu.VMEM((groups, rows // 2, width), jnp.float32),
            pltpu.VMEM((groups, rows // 2, width), jnp.bfloat16),
            pltpu.VMEM((groups, rows // 2, width), jnp.bfloat16),
            pltpu.VMEM((groups, rows, width), jnp.bfloat16),
            dma((lon_size - 1,)),
            dma((lon_size - 1,)),
            dma((lon_size - 1,)),
            dma((lon_size - 1,)),
            dma((groups, levels)),
            dma((groups, levels)),
            dma((groups, levels)),
            dma((groups, levels)),
            dma((6,)),
            dma((6,)),
        ],
        compiler_params=pltpu.CompilerParams(
            collective_id=0, has_side_effects=True, vmem_limit_bytes=40 * 1024 * 1024
        ),
        cost_estimate=pl.CostEstimate(
            flops=flops, bytes_accessed=2 * slots * lat_rows * degrees, transcendentals=0
        ),
    )(parts, legendre, load[None, :], *edges)


def on_device(elevation, depth, friction, land_mask, order_map, legendre, load):
    channels, lat_rows, lon_cols = elevation.shape
    slot_count = legendre.shape[0]
    band_count = lax.axis_size("lat")
    sector_count = lax.axis_size("lon")
    lat_count = lat_rows * band_count
    lon_count = lon_cols * sector_count
    band = lax.axis_index("lat")
    lat_start = band * lat_rows
    col_start = lax.axis_index("lon") * lon_cols
    sea_mask = land_mask.astype(jnp.float32)
    sea_depth = depth * sea_mask

    steps = jnp.arange(lon_cols + 128, dtype=jnp.int32)
    steps = jnp.where(steps == lon_cols + 127, -1, steps)
    columns = (col_start + steps + lon_count) % lon_count
    basis = fourier_basis(order_map, columns, lon_count)
    longitude = columns.astype(jnp.float32) * (2.0 * math.pi / lon_count)
    waves = jnp.stack(
        [jnp.cos(2.0 * longitude), jnp.sin(2.0 * longitude), jnp.cos(longitude), jnp.sin(longitude)]
    )
    lines = jnp.arange(lat_rows + 8, dtype=jnp.int32)
    lines = lat_start + jnp.where(lines == lat_rows + 7, -1, lines)
    lat_step = 2.0 * LAT_EDGE / lat_count
    latitude = -LAT_EDGE + (lines.astype(jnp.float32) + 0.5) * lat_step
    face_latitude = -LAT_EDGE + (lines.astype(jnp.float32) + 1.0) * lat_step
    lat_table = jnp.stack(
        [
            jnp.cos(latitude) ** 2,
            jnp.sin(2.0 * latitude),
            1.0 / jnp.cos(latitude),
            jnp.cos(face_latitude),
        ],
        axis=1,
    )
    poles = jnp.stack([band < band_count - 1, band > 0]).astype(jnp.float32)

    leg_edges = jnp.stack([legendre[:, 0], legendre[:, -1]])
    row_edges = jnp.stack(
        [
            jnp.concatenate([elevation[:, j], sea_depth[None, j], friction[None, j]], axis=0)
            for j in (0, lat_rows - 1)
        ]
    )
    col_edges = jnp.concatenate(
        [
            jnp.pad(
                jnp.concatenate([elevation[:, :, i], sea_depth[None, :, i], friction[None, :, i]]),
                ((0, 62 - channels), (0, 0)),
            )
            for i in (0, lon_cols - 1)
        ]
    ).T

    flat_field = (elevation * sea_mask).reshape(channels * lat_rows, lon_cols)
    product = lax.dot_general(
        basis[:, :lon_cols],
        flat_field,
        (((1,), (1,)), ((), ())),
        precision=PRECISE,
        preferred_element_type=jnp.float32,
    )
    parts = product.reshape(sector_count, slot_count, 2 * channels, lat_rows)
    blocks, row_halo, col_halo = transform(
        parts, legendre, load, (leg_edges, row_edges, col_edges), band_count, sector_count
    )
    synth = blocks[:, :, : lat_rows + 8].reshape(-1, 2, channels, lat_rows + 8)
    synth = synth.transpose(2, 3, 0, 1).reshape(channels, lat_rows + 8, basis.shape[0])
    return tuple(
        sweep(
            elevation,
            depth,
            friction,
            land_mask,
            (row_halo, col_halo),
            synth,
            basis,
            lat_table,
            waves,
            poles,
        )
    )


def solution(mesh):
    return jax.shard_map(
        on_device,
        mesh=mesh,
        in_specs=(
            P(None, "lat", "lon"),
            P("lat", "lon"),
            P("lat", "lon"),
            P("lat", "lon"),
            P(),
            P("lon", "lat", None),
            P(),
        ),
        out_specs=(P(None, "lat", "lon"), P(None, "lat", "lon"), P("lat", "lon")),
        check_vma=False,
    )
```

profile of v0, /device:TPU:13, one launch (start us, length us, event | category | flops | bytes accessed | tf_op | source)
XLA Modules:
  0.0 112.7 jit_solution(14625992066599819275)
XLA Ops:
  0.6 0.0 copy-start
  0.7 0.1 add_convert_fusion.pole_ref
  0.7 0.8 compare_select_fusion.5
  1.5 1.0 slice_reduce_fusion.3
  2.5 0.1 add_cosine_fusion
  2.6 0.1 broadcast_divide_fusion
  2.6 0.7 fusion.21
  3.4 0.1 multiply_sine_fusion.2
  3.5 0.1 multiply_sine_fusion.1
  3.6 0.8 multiply_cosine_fusion
  4.4 0.1 copy.59.weight_ref
  4.5 0.1 copy.58.lat_ref
  4.6 1.1 fusion.19
  5.7 1.0 convert_multiply_fusion
  6.7 0.2 slice_reduce_fusion.1
  6.9 0.9 convert_element_type.70
  7.9 1.1 cosine_multiply_fusion
  8.9 0.1 copy.47
  9.1 0.1 reshape.409.basis_ref
  9.2 1.4 %fusion.17 = (bf16[16,1,2048]{2,1,0:T(2,128)(2,1)S(1)}, bf16[16,1,2048]{2,1,0:T(2,128)(2,1)S(1)}) fusion(bf16[16,64,2048]{2,1,0:T(8,128)(2,1)} %leg_ref.1), kind=kLoop, calls=%fused_computation.69 | loop fusion | bytes 262144 | tf_op jit(solution)/shard_map/slice | solution.py:564
  10.6 0.1 copy_bitcast_fusion
  10.7 0.0 copy-done
  10.7 1.0 fusion.18
  11.7 1.2 %copy.64 = f32[16,64,1]{1,0,2:T(8,128)S(1)} copy(f32[16,64,1]{2,1,0:T(8,128)} %get-tuple-element.15) | data formatting | bytes 8192
  13.0 0.2 copy.65
  13.2 0.1 copy.55
  13.3 0.1 copy.53
  13.4 0.1 fusion.5.col_edges_ref
  13.5 0.3 broadcast_multiply_fusion
  13.8 0.0 copy-start.10
  13.8 2.1 %fusion = f32[64,1024]{1,0:T(8,128)S(1)} fusion(f32[1024,512]{1,0:T(8,128)S(1)} %bitcast.36, f32[64,640]{1,0:T(8,128)S(1)} %reshape.409.basis_ref), kind=kOutput, calls=%fused_computation.5 | convolution fusion | flops 402653184 | bytes 2490368 | tf_op jit(solution)/shard_map/dot_general | solution.py:582
  15.9 0.1 reshape.411.part_ref
  16.0 0.0 copy-done.10
  16.1 0.0 copy-start.1
  16.1 2.2 %copy-done.1 = bf16[16,64,2048]{2,1,0:T(8,128)(2,1)S(1)} copy-done((bf16[16,64,2048]{2,1,0:T(8,128)(2,1)S(1)}, bf16[16,64,2048]{2,1,0:T(8,128)(2,1)}, u32[]{:S(2)}) %copy-start.1) | copy-done | bytes 4194328
  18.2 0.0 copy-start.2
  18.2 0.0 copy-start.3
  18.3 0.0 copy-start.5
  18.3 0.0 copy-start.11
  18.3 0.0 copy-start.12
  18.3 66.7 %shard_map.121 = (f32[32,32,128]{2,1,0:T(8,128)S(1)}, f32[2,18,512]{2,1,0:T(8,128)S(1)}, f32[2,64,128]{2,1,0:T(8,128)S(1)}) custom-call(f32[2,16,32,64]{3,2,1,0:T(8,128)S(1)} %reshape.411.part_ref, bf16[16,64,2048]{2,1,0:T(8,128)(2,1)S(1)} %copy-done.1, f32[1,2048]{1,0:T(1,128)S(1)} %bitcast.35, bf16[2,16,2048]{2,1,0:T(8,128)(2,1)S(1)} %pad_maximum_fusion.1.leg_edges_ref, ...), custom_call_target="tpu_custom_call" | custom-call | flops 268435456 | bytes 4194304 | tf_op jit(solution)/shard_map/pallas_call | solution.py:487
  85.0 0.0 copy-start.4
  85.0 0.8 copy-done.4
  85.8 0.0 copy-start.6
  85.8 0.6 copy-done.6
  86.4 0.0 copy-start.8
  86.4 0.6 copy-done.8
  87.1 1.3 %copy.57.synth_ref = f32[16,72,64]{2,1,0:T(8,128)S(1)} copy(f32[16,72,64]{1,0,2:T(8,128)} %bitcast.34) | data formatting | bytes 589824 | tf_op jit(solution)/shard_map/reshape | solution.py:594
  88.4 0.0 copy-done.2
  88.4 0.0 copy-done.3
  88.4 0.0 copy-done.5
  88.4 0.0 copy-done.11
  88.4 0.0 copy-done.12
  88.4 0.0 copy-start.7
  88.4 0.9 copy-done.7
  89.3 0.0 copy-start.9
  89.3 0.8 copy-done.9
  90.1 22.5 %shard_map.122 = (f32[16,64,512]{2,1,0:T(8,128)}, f32[16,64,512]{2,1,0:T(8,128)}, f32[64,512]{1,0:T(8,128)}) custom-call(f32[8]{0:T(128)S(1)} %copy-done.11, f32[8]{0:T(128)S(1)} %copy-done.12, f32[2]{0:T(128)S(1)} %add_convert_fusion.pole_ref, f32[16,64,512]{2,1,0:T(8,128)S(1)} %copy-done, f32[64,512]{1,0:T(8,128)S(1)} %copy-done.3, ...), custom_call_target="tpu_custom_call" | custom-call | tf_op jit(solution)/shard_map/pallas_call | solution.py:185
  (15 shorter events, 0.2 us)
Async XLA Ops:
  0.6 10.1 %copy-start = (f32[16,64,512]{2,1,0:T(8,128)S(1)}, f32[16,64,512]{2,1,0:T(8,128)}, u32[]{:S(2)}) copy-start(f32[16,64,512]{2,1,0:T(8,128)} %elev_ref.1) | copy-start | bytes 6291460
  13.8 2.3 %copy-start.10 = (f32[2048]{0:T(1024)S(1)}, f32[2048]{0:T(1024)}, u32[]{:S(2)}) copy-start(f32[2048]{0:T(1024)} %param.16) | copy-start | bytes 24580
  16.1 2.2 %copy-start.1 = (bf16[16,64,2048]{2,1,0:T(8,128)(2,1)S(1)}, bf16[16,64,2048]{2,1,0:T(8,128)(2,1)}, u32[]{:S(2)}) copy-start(bf16[16,64,2048]{2,1,0:T(8,128)(2,1)} %leg_ref.1) | copy-start | bytes 12582916
  18.2 70.1 %copy-start.2 = (s32[64,512]{1,0:T(8,128)S(1)}, s32[64,512]{1,0:T(8,128)}, u32[]{:S(2)}) copy-start(s32[64,512]{1,0:T(8,128)} %mask_ref.1) | copy-start | bytes 393220
  18.2 70.1 %copy-start.3 = (f32[64,512]{1,0:T(8,128)S(1)}, f32[64,512]{1,0:T(8,128)}, u32[]{:S(2)}) copy-start(f32[64,512]{1,0:T(8,128)} %depth_ref.1) | copy-start | bytes 393220
  18.3 70.1 %copy-start.5 = (f32[64,512]{1,0:T(8,128)S(1)}, f32[64,512]{1,0:T(8,128)}, u32[]{:S(2)}) copy-start(f32[64,512]{1,0:T(8,128)} %drag_ref.1) | copy-start | bytes 393220
  18.3 70.1 %copy-start.11 = (f32[8]{0:T(128)S(1)}, f32[8]{0:T(128)}, u32[]{:S(2)}) copy-start(f32[8]{0:T(128)} %constant.74.clone.omega_ref) | copy-start | bytes 100
  18.3 70.1 %copy-start.12 = (f32[8]{0:T(128)S(1)}, f32[8]{0:T(128)}, u32[]{:S(2)}) copy-start(f32[8]{0:T(128)} %constant.75.clone.amp_ref) | copy-start | bytes 100
  85.0 0.8 copy-start.4
  85.8 0.6 copy-start.6
  86.4 0.6 copy-start.8
  88.4 0.9 copy-start.7
  89.3 0.8 copy-start.9
where the time goes:
time: 113 us
  Pallas kernels  89.3 us (79%)
  local copies, waits for them, and re-layouts  14.9 us (13%)
  other arithmetic  5.42 us (5%)
  matrix products  2.14 us (2%)
    pallas_call x1, Pallas kernels, transform(): pl.pallas_call(functools.partial(transform_kernel, lat_size, lon_size, gr...  66.7 us
    pallas_call x1, Pallas kernels, sweep(): pl.pallas_call(sweep_kernel, grid=(channels // 2,), out_shape=[jax.ShapeD...  22.5 us
    unnamed x30, local copies, waits for them, and re-layouts  7.46 us

commit v1 on v0

--- a/solution.py
+++ b/solution.py
@@ -164,7 +164,7 @@
                 preferred_element_type=jnp.float32,
             )
 
-        @pl.loop(0, lat_rows)
+        @pl.loop(0, lat_rows, unroll=UNROLL)
         def _(j):
             east, north = sampled(east_cells[j]), sampled(north_cells[j])
             squares = east * east + north * north + SPEED_EPS * SPEED_EPS
@@ -178,6 +178,9 @@
     wide_rows, wide_cols = lat_rows + 8, lon_cols + 128
     whole = pl.BlockSpec(memory_space=pltpu.VMEM)
     scalars = pl.BlockSpec(memory_space=pltpu.SMEM)
+
+    def fixed(value):
+        return pl.BlockSpec(value.shape, lambda k: (0,) * value.ndim)
 
     def pair(*shape):
         return pl.BlockSpec((2,) + shape, lambda k: (k, 0, 0))
@@ -192,9 +195,9 @@
         ],
         in_specs=[scalars] * 3
         + [pair(lat_rows, lon_cols)]
-        + [whole] * 5
+        + [fixed(value) for value in (depth, friction, land_mask) + halos]
         + [pair(wide_rows, basis.shape[0])]
-        + [whole] * 4,
+        + [fixed(basis), fixed(lat_table), fixed(waves), whole],
         out_specs=[
             pair(lat_rows, lon_cols),
             pair(lat_rows, lon_cols),
@@ -226,32 +229,51 @@
 
 
 GROUPS = 4
+UNROLL = 16
 MESH = pl.DeviceIdType.MESH
 
 
+def lat_factors(lat_size):
+    return (2, lat_size // 8, 4)
+
+
 def transform_kernel(
-    lat_size,
+    factors,
     lon_size,
     groups,
     part_ref,
-    leg_ref,
+    leg_hbm,
     load_ref,
     leg_edges_ref,
-    row_edges_ref,
-    col_edges_ref,
+    elev_hbm,
+    depth_hbm,
+    drag_hbm,
+    mask_hbm,
     out_ref,
     row_halo_ref,
     col_halo_ref,
-    sector_parts,
+    leg_ref,
+    row_strips,
+    col_strips,
+    row_masks,
+    col_masks,
+    row_edges,
+    col_edges,
+    packed_out,
+    packed_in,
     fourier,
     leg_halo,
     synth,
     synth_edges,
+    packed_synth,
+    packed_edges,
     acc,
     first_recv,
     rs_send,
     rs_recv,
     gathered,
+    leg_sem,
+    strip_sem,
     lon_send,
     lon_recv,
     out_send,
@@ -265,32 +287,58 @@
 ):
     lat_me = lax.axis_index("lat")
     lon_me = lax.axis_index("lon")
-    levels = lat_size.bit_length() - 1
+    lat_size = math.prod(factors)
+    phases = len(factors)
     slots, lat_rows, degrees = leg_ref.shape
     quantities = part_ref.shape[2]
+    channels = elev_hbm.shape[0]
+    lon_cols = elev_hbm.shape[2]
     rows = slots * quantities
     width = degrees // groups
-    bits = [(lat_me // 2**k) % 2 for k in range(levels)]
-    partners = [lat_me + (1 - 2 * bits[k]) * 2**k for k in range(levels)]
+    pairs = slots // 2
+
+    loads = [pltpu.make_async_copy(leg_hbm, leg_ref, leg_sem.at[0])]
+    for side in range(2):
+        top, first = side * (lat_rows - 8), side * (lon_cols - 128)
+        for n, (field, row_to, col_to) in enumerate(
+            (
+                (elev_hbm, row_strips.at[side, :channels], col_strips.at[side, :channels]),
+                (depth_hbm, row_strips.at[side, channels], col_strips.at[side, channels]),
+                (drag_hbm, row_strips.at[side, channels + 1], col_strips.at[side, channels + 1]),
+                (mask_hbm, row_masks.at[side], col_masks.at[side]),
+            )
+        ):
+            lead = (slice(None),) if n == 0 else ()
+            row_from = field.at[lead + (pl.ds(top, 8), slice(None))]
+            col_from = field.at[lead + (slice(None), pl.ds(first, 128))]
+            loads.append(pltpu.make_async_copy(row_from, row_to, strip_sem.at[side, n]))
+            loads.append(pltpu.make_async_copy(col_from, col_to, strip_sem.at[side, 4 + n]))
+    for copy in loads[1:] + loads[:1]:
+        copy.start()
+
+    digits, peers, kept, sizes = [], [], [0], [rows]
+    stride = 1
+    for factor in factors:
+        digit = (lat_me // stride) % factor
+        around = [(digit + d) % factor for d in range(1, factor)]
+        digits.append(digit)
+        peers.append([(other, lat_me + (other - digit) * stride) for other in around])
+        sizes.append(sizes[-1] // factor)
+        kept.append(pl.multiple_of(kept[-1] + digit * sizes[-1], sizes[-1]))
+        stride *= factor
     others = [lax.rem(lon_me + d, lon_size) for d in range(1, lon_size)]
-    kept, sent = [0], []
-    for k in range(levels):
-        half = rows >> (k + 1)
-        sent.append(pl.multiple_of(kept[k] + (1 - bits[k]) * half, half))
-        kept.append(pl.multiple_of(kept[k] + bits[k] * half, half))
-
-    barrier = pltpu.get_barrier_semaphore()
-    for k in range(levels):
-        pl.semaphore_signal(
-            barrier, inc=1, device_id=(partners[k], lon_me), device_id_type=MESH
-        )
-    for other in others:
-        pl.semaphore_signal(barrier, inc=1, device_id=(lat_me, other), device_id_type=MESH)
     above, below = lax.rem(lat_me + lat_size - 1, lat_size), lax.rem(lat_me + 1, lat_size)
     left, right = lax.rem(lon_me + lon_size - 1, lon_size), lax.rem(lon_me + 1, lon_size)
-    for near in (above, below):
-        pl.semaphore_signal(barrier, inc=1, device_id=(near, lon_me), device_id_type=MESH)
-    pl.semaphore_wait(barrier, levels + lon_size + 1)
+
+    barrier = pltpu.get_barrier_semaphore()
+    greeted = [(other, lon_me) for phase in peers for _, other in phase]
+    greeted += [(above, lon_me), (below, lon_me)] + [(lat_me, other) for other in others]
+    for device in greeted:
+        pl.semaphore_signal(barrier, inc=1, device_id=device, device_id_type=MESH)
+    for d, other in enumerate(others):
+        packed_out[d, :, :, :lat_rows] = part_ref[other, :pairs]
+        packed_out[d, :, :, lat_rows:] = part_ref[other, pairs:]
+    pl.semaphore_wait(barrier, len(greeted))
 
     pending = []
 
@@ -308,40 +356,55 @@
         return copy
 
     copies = [
-        send(
-            part_ref.at[other],
-            sector_parts.at[d],
-            lon_send.at[d],
-            lon_recv.at[d],
-            (lat_me, other),
-        )
+        send(packed_out.at[d], packed_in.at[d], lon_send.at[d], lon_recv.at[d], (lat_me, other))
         for d, other in enumerate(others)
     ]
+
+    for copy in loads[1:]:
+        copy.wait()
+    lane = lax.broadcasted_iota(jnp.int32, (lat_rows, 128), 1)
+    edge_cols = jnp.zeros((lat_rows, 128), jnp.float32)
+    for side in range(2):
+        row, col = 7 * side, 127 * side
+        for field in range(channels + 2):
+            line = row_strips[side, field, row : row + 1, :]
+            column = col_strips[side, field, :, col : col + 1]
+            if field == channels:
+                line = line * row_masks[side, row : row + 1, :].astype(jnp.float32)
+                column = column * col_masks[side, :, col : col + 1].astype(jnp.float32)
+            row_edges[side, field : field + 1, :] = line
+            edge_cols = jnp.where(lane == 64 * side + field, column, edge_cols)
+    col_edges[...] = edge_cols
     halos = [
         send(source, target, halo_send.at[n], halo_recv.at[n], device)
         for n, (source, target, device) in enumerate(
             (
                 (leg_edges_ref.at[0], leg_halo.at[pl.ds(0, slots)], (above, lon_me)),
                 (leg_edges_ref.at[1], leg_halo.at[pl.ds(slots, slots)], (below, lon_me)),
-                (row_edges_ref.at[0], row_halo_ref.at[0], (above, lon_me)),
-                (row_edges_ref.at[1], row_halo_ref.at[1], (below, lon_me)),
-                (col_edges_ref, col_halo_ref.at[0], (lat_me, left)),
-                (col_edges_ref, col_halo_ref.at[1], (lat_me, right)),
+                (row_edges.at[0], row_halo_ref.at[0], (above, lon_me)),
+                (row_edges.at[1], row_halo_ref.at[1], (below, lon_me)),
+                (col_edges, col_halo_ref.at[0], (lat_me, left)),
+                (col_edges, col_halo_ref.at[1], (lat_me, right)),
             )
         )
     ]
     for copy in copies:
         copy.wait_recv()
-    total = part_ref[lon_me]
-    for d in range(lon_size - 1):
-        total = total + sector_parts[d]
-    fourier[...] = total.astype(jnp.bfloat16)
+    for half in range(2):
+        total = part_ref[lon_me, half * pairs : (half + 1) * pairs]
+        for d in range(lon_size - 1):
+            total = total + packed_in[d, :, :, half * lat_rows : (half + 1) * lat_rows]
+        fourier[half * pairs : (half + 1) * pairs] = total.astype(jnp.bfloat16)
+    loads[0].wait()
 
     reducing = {}
     gathering = {}
+    offsets = [0, 0]
+    for p in range(1, phases):
+        offsets.append(offsets[-1] + (factors[p] - 1) * sizes[p + 1])
 
     def analyse(g):
-        @pl.loop(0, slots)
+        @pl.loop(0, slots, unroll=UNROLL)
         def _(s):
             acc[g, pl.ds(pl.multiple_of(s * quantities, quantities), quantities), :] = jnp.dot(
                 fourier[s],
@@ -349,61 +412,70 @@
                 preferred_element_type=jnp.float32,
             )
 
-        reducing[g] = send(
-            acc.at[g, pl.ds(sent[0], rows // 2), :],
-            first_recv.at[g],
-            red_send.at[g, 0],
-            red_recv.at[g, 0],
-            (partners[0], lon_me),
-        )
-
-    def offset_of(k):
-        return rows // 2 - (rows >> k)
-
-    def reduce(g, k):
-        reducing[g].wait_recv()
-        size = rows >> (k + 1)
-
-        def arrived(start, count):
-            if k == 0:
-                return first_recv[g, pl.ds(start, count), :]
-            return rs_recv[g, pl.ds(offset_of(k) + start, count), :].astype(jnp.float32)
-
-        if k < levels - 1:
-            half = size // 2
-            away = pl.multiple_of((1 - bits[k + 1]) * half, half)
-            home = pl.multiple_of(bits[k + 1] * half, half)
-            place = pl.ds(offset_of(k + 1), half)
-            rs_send[g, place, :] = (
-                acc[g, pl.ds(sent[k + 1], half), :] + arrived(away, half)
-            ).astype(jnp.bfloat16)
-            reducing[g] = send(
-                rs_send.at[g, place, :],
-                rs_recv.at[g, place, :],
-                red_send.at[g, k + 1],
-                red_recv.at[g, k + 1],
-                (partners[k + 1], lon_me),
-            )
-            acc[g, pl.ds(kept[k + 1 + 1], half), :] = acc[
-                g, pl.ds(kept[k + 1 + 1], half), :
-            ] + arrived(home, half)
+        away = pl.multiple_of(peers[0][0][0] * sizes[1], sizes[1])
+        reducing[g] = [
+            send(
+                acc.at[g, pl.ds(away, sizes[1]), :],
+                first_recv.at[g],
+                red_send.at[g, 0, 0],
+                red_recv.at[g, 0, 0],
+                (peers[0][0][1], lon_me),
+            )
+        ]
+
+    def reduce(g, p):
+        for copy in reducing[g]:
+            copy.wait_recv()
+        size = sizes[p + 1]
+
+        def value(start, count):
+            total = acc[g, pl.ds(pl.multiple_of(kept[p + 1] + start, count), count), :]
+            if p == 0:
+                return total + first_recv[g, pl.ds(start, count), :]
+            for d in range(factors[p] - 1):
+                place = pl.multiple_of(offsets[p] + d * size + start, 16)
+                total = total + rs_recv[g, pl.ds(place, count), :].astype(jnp.float32)
+            return total
+
+        if p < phases - 1:
+            sub = sizes[p + 2]
+            reducing[g] = []
+            for d, (digit, device) in enumerate(peers[p + 1]):
+                place = pl.ds(offsets[p + 1] + d * sub, sub)
+                rs_send[g, place, :] = value(pl.multiple_of(digit * sub, sub), sub).astype(
+                    jnp.bfloat16
+                )
+                reducing[g].append(
+                    send(
+                        rs_send.at[g, place, :],
+                        rs_recv.at[g, place, :],
+                        red_send.at[g, p + 1, d],
+                        red_recv.at[g, p + 1, d],
+                        (device, lon_me),
+                    )
+                )
+            acc[g, pl.ds(kept[p + 2], sub), :] = value(
+                pl.multiple_of(digits[p + 1] * sub, sub), sub
+            )
         else:
-            mine = pl.ds(kept[levels], size)
             scale = load_ref[:, g * width : (g + 1) * width]
-            gathered[g, mine, :] = ((acc[g, mine, :] + arrived(0, size)) * scale).astype(
+            gathered[g, pl.ds(kept[phases], size), :] = (value(0, size) * scale).astype(
                 jnp.bfloat16
             )
-            spread(g, levels - 1)
-
-    def spread(g, k):
-        held = pl.ds(kept[k + 1], rows >> (k + 1))
-        gathering[g] = send(
-            gathered.at[g, held, :],
-            gathered.at[g, held, :],
-            gat_send.at[g, k],
-            gat_recv.at[g, k],
-            (partners[k], lon_me),
-        )
+            spread(g, phases - 1)
+
+    def spread(g, p):
+        held = pl.ds(kept[p + 1], sizes[p + 1])
+        gathering[g] = [
+            send(
+                gathered.at[g, held, :],
+                gathered.at[g, held, :],
+                gat_send.at[g, p, d],
+                gat_recv.at[g, p, d],
+                (device, lon_me),
+            )
+            for d, (_, device) in enumerate(peers[p])
+        ]
 
     def synthesise(g):
         if g == 0:
@@ -420,7 +492,7 @@
         else:
             synth_edges[...] = synth_edges[...] + at_edges
 
-        @pl.loop(0, slots)
+        @pl.loop(0, slots, unroll=UNROLL)
         def _(s):
             part = lax.dot_general(
                 gathered[g, pl.ds(pl.multiple_of(s * quantities, quantities), quantities), :],
@@ -433,85 +505,127 @@
             else:
                 synth[s] = synth[s] + part
 
-    def gather(g, k):
-        gathering[g].wait_recv()
-        if k > 0:
-            spread(g, k - 1)
+    def gather(g, p):
+        for copy in gathering[g]:
+            copy.wait_recv()
+        if p > 0:
+            spread(g, p - 1)
         else:
             synthesise(g)
 
-    for wave in range(groups + 2 * levels):
+    for wave in range(groups + 2 * phases):
         for g in range(groups):
             stage = wave - g
             if stage == 0:
                 analyse(g)
-            elif 1 <= stage <= levels:
+            elif 1 <= stage <= phases:
                 reduce(g, stage - 1)
-            elif levels < stage <= 2 * levels:
-                gather(g, 2 * levels - stage)
-
-    lanes = lax.broadcasted_iota(jnp.int32, (quantities, 2 * slots), 1)
+            elif phases < stage <= 2 * phases:
+                gather(g, 2 * phases - stage)
+
+    packed_synth[lon_me, :, :, :lat_rows] = synth[:pairs]
+    packed_synth[lon_me, :, :, lat_rows:] = synth[pairs:]
+    edge_lane = lax.broadcasted_iota(jnp.int32, (quantities, 2 * slots), 1) % slots
+    edges = jnp.zeros((quantities, 2 * slots), jnp.float32)
+    for s in range(slots):
+        edges = jnp.where(
+            edge_lane == s, synth_edges[s * quantities : (s + 1) * quantities, :], edges
+        )
+    packed_edges[lon_me] = edges
+    copies = []
+    for d, other in enumerate(others):
+        for n, array in enumerate((packed_synth, packed_edges)):
+            copies.append(
+                send(
+                    array.at[lon_me],
+                    array.at[lon_me],
+                    out_send.at[d, n],
+                    out_recv.at[d, n],
+                    (lat_me, other),
+                )
+            )
     places = lax.broadcasted_iota(jnp.int32, (quantities, out_ref.shape[2] - lat_rows), 1)
 
-    @pl.loop(0, slots)
-    def _(s):
-        edges = synth_edges[pl.ds(pl.multiple_of(s * quantities, quantities), quantities), :]
-        after = jnp.sum(jnp.where(lanes == s, edges, 0.0), axis=1, keepdims=True)
-        before = jnp.sum(jnp.where(lanes == slots + s, edges, 0.0), axis=1, keepdims=True)
-        out_ref[lon_me * slots + s, :, :lat_rows] = synth[s]
-        out_ref[lon_me * slots + s, :, lat_rows:] = jnp.where(
-            places == 0, after, jnp.where(places == 7, before, 0.0)
-        )
-
-    block = out_ref.at[pl.ds(lon_me * slots, slots)]
-    copies = [
-        send(block, block, out_send.at[d], out_recv.at[d], (lat_me, other))
-        for d, other in enumerate(others)
-    ]
+    def unpack(block):
+        both = packed_edges[block]
+        for s in range(slots):
+            slot = block * slots + s
+            half = s // pairs
+            out_ref[slot, :, :lat_rows] = packed_synth[
+                block, s % pairs, :, half * lat_rows : (half + 1) * lat_rows
+            ]
+            out_ref[slot, :, lat_rows:] = jnp.where(
+                places == 0,
+                both[:, s : s + 1],
+                jnp.where(places == 7, both[:, slots + s : slots + s + 1], 0.0),
+            )
+
+    unpack(lon_me)
     for copy in copies + halos[2:]:
         copy.wait_recv()
+    for other in others:
+        unpack(other)
     for copy in pending:
         copy.wait_send()
 
 
-def transform(parts, legendre, load, edges, lat_size, lon_size):
+def transform(parts, legendre, load, leg_edges, fields, lat_size, lon_size):
     slots, lat_rows, degrees = legendre.shape
     quantities = parts.shape[2]
+    channels, _, lon_cols = fields[0].shape
     rows = slots * quantities
     groups = GROUPS
     width = degrees // groups
-    levels = lat_size.bit_length() - 1
+    factors = lat_factors(lat_size)
+    staged, size = 0, rows // factors[0]
+    for factor in factors[1:]:
+        size //= factor
+        staged += (factor - 1) * size
     vmem = pl.BlockSpec(memory_space=pltpu.VMEM)
+    anywhere = pl.BlockSpec(memory_space=pl.ANY)
     dma = pltpu.SemaphoreType.DMA
-    flops = 4 * rows * lat_rows * degrees
+    most = (groups, len(factors), max(factors) - 1)
+    f32, bf16 = jnp.float32, jnp.bfloat16
     return pl.pallas_call(
-        functools.partial(transform_kernel, lat_size, lon_size, groups),
+        functools.partial(transform_kernel, factors, lon_size, groups),
         out_shape=[
-            jax.ShapeDtypeStruct((lon_size * slots, quantities, 128), jnp.float32),
-            jax.ShapeDtypeStruct(edges[1].shape, jnp.float32),
-            jax.ShapeDtypeStruct((2,) + edges[2].shape, jnp.float32),
+            jax.ShapeDtypeStruct((lon_size * slots, quantities, 128), f32),
+            jax.ShapeDtypeStruct((2, channels + 2, lon_cols), f32),
+            jax.ShapeDtypeStruct((2, lat_rows, 128), f32),
         ],
-        in_specs=[vmem] * 6,
+        in_specs=[vmem, anywhere, vmem, vmem] + [anywhere] * 4,
         out_specs=[vmem] * 3,
         scratch_shapes=[
-            pltpu.VMEM((lon_size - 1, slots, quantities, lat_rows), jnp.float32),
-            pltpu.VMEM((slots, quantities, lat_rows), jnp.bfloat16),
-            pltpu.VMEM((2 * slots, degrees), jnp.bfloat16),
-            pltpu.VMEM((slots, quantities, lat_rows), jnp.float32),
-            pltpu.VMEM((rows, 2 * slots), jnp.float32),
-            pltpu.VMEM((groups, rows, width), jnp.float32),
-            pltpu.VMEM((groups, rows // 2, width), jnp.float32),
-            pltpu.VMEM((groups, rows // 2, width), jnp.bfloat16),
-            pltpu.VMEM((groups, rows // 2, width), jnp.bfloat16),
-            pltpu.VMEM((groups, rows, width), jnp.bfloat16),
+            pltpu.VMEM(legendre.shape, bf16),
+            pltpu.VMEM((2, channels + 2, 8, lon_cols), f32),
+            pltpu.VMEM((2, channels + 2, lat_rows, 128), f32),
+            pltpu.VMEM((2, 8, lon_cols), jnp.int32),
+            pltpu.VMEM((2, lat_rows, 128), jnp.int32),
+            pltpu.VMEM((2, channels + 2, lon_cols), f32),
+            pltpu.VMEM((lat_rows, 128), f32),
+            pltpu.VMEM((lon_size - 1, slots // 2, quantities, 2 * lat_rows), f32),
+            pltpu.VMEM((lon_size - 1, slots // 2, quantities, 2 * lat_rows), f32),
+            pltpu.VMEM((slots, quantities, lat_rows), bf16),
+            pltpu.VMEM((2 * slots, degrees), bf16),
+            pltpu.VMEM((slots, quantities, lat_rows), f32),
+            pltpu.VMEM((rows, 2 * slots), f32),
+            pltpu.VMEM((lon_size, slots // 2, quantities, 2 * lat_rows), f32),
+            pltpu.VMEM((lon_size, quantities, 2 * slots), f32),
+            pltpu.VMEM((groups, rows, width), f32),
+            pltpu.VMEM((groups, rows // 2, width), f32),
+            pltpu.VMEM((groups, staged, width), bf16),
+            pltpu.VMEM((groups, staged, width), bf16),
+            pltpu.VMEM((groups, rows, width), bf16),
+            dma((1,)),
+            dma((2, 8)),
             dma((lon_size - 1,)),
             dma((lon_size - 1,)),
-            dma((lon_size - 1,)),
-            dma((lon_size - 1,)),
-            dma((groups, levels)),
-            dma((groups, levels)),
-            dma((groups, levels)),
-            dma((groups, levels)),
+            dma((lon_size - 1, 2)),
+            dma((lon_size - 1, 2)),
+            dma(most),
+            dma(most),
+            dma(most),
+            dma(most),
             dma((6,)),
             dma((6,)),
         ],
@@ -519,9 +633,11 @@
             collective_id=0, has_side_effects=True, vmem_limit_bytes=40 * 1024 * 1024
         ),
         cost_estimate=pl.CostEstimate(
-            flops=flops, bytes_accessed=2 * slots * lat_rows * degrees, transcendentals=0
+            flops=4 * rows * lat_rows * degrees,
+            bytes_accessed=2 * slots * lat_rows * degrees,
+            transcendentals=0,
         ),
-    )(parts, legendre, load[None, :], *edges)
+    )(parts, legendre, load[None, :], leg_edges, *fields)
 
 
 def on_device(elevation, depth, friction, land_mask, order_map, legendre, load):
@@ -535,7 +651,6 @@
     lat_start = band * lat_rows
     col_start = lax.axis_index("lon") * lon_cols
     sea_mask = land_mask.astype(jnp.float32)
-    sea_depth = depth * sea_mask
 
     steps = jnp.arange(lon_cols + 128, dtype=jnp.int32)
     steps = jnp.where(steps == lon_cols + 127, -1, steps)
@@ -562,22 +677,6 @@
     poles = jnp.stack([band < band_count - 1, band > 0]).astype(jnp.float32)
 
     leg_edges = jnp.stack([legendre[:, 0], legendre[:, -1]])
-    row_edges = jnp.stack(
-        [
-            jnp.concatenate([elevation[:, j], sea_depth[None, j], friction[None, j]], axis=0)
-            for j in (0, lat_rows - 1)
-        ]
-    )
-    col_edges = jnp.concatenate(
-        [
-            jnp.pad(
-                jnp.concatenate([elevation[:, :, i], sea_depth[None, :, i], friction[None, :, i]]),
-                ((0, 62 - channels), (0, 0)),
-            )
-            for i in (0, lon_cols - 1)
-        ]
-    ).T
-
     flat_field = (elevation * sea_mask).reshape(channels * lat_rows, lon_cols)
     product = lax.dot_general(
         basis[:, :lon_cols],
@@ -588,7 +687,13 @@
     )
     parts = product.reshape(sector_count, slot_count, 2 * channels, lat_rows)
     blocks, row_halo, col_halo = transform(
-        parts, legendre, load, (leg_edges, row_edges, col_edges), band_count, sector_count
+        parts,
+        legendre,
+        load,
+        leg_edges,
+        (elevation, depth, friction, land_mask),
+        band_count,
+        sector_count,
     )
     synth = blocks[:, :, : lat_rows + 8].reshape(-1, 2, channels, lat_rows + 8)
     synth = synth.transpose(2, 3, 0, 1).reshape(channels, lat_rows + 8, basis.shape[0])

time: 113 us -> 90.2 us (0.80); the launches traced: 113 us -> 88.5 us
  Pallas kernels: 89.3 us -> 70.1 us
  local copies, waits for them, and re-layouts: 14.9 us -> 9.95 us
    pallas_call x1, Pallas kernels: 66.7 us -> 56.6 us  [transform(): pl.pallas_call(functools.partial(transform_kernel, factors, lon_size, gro...]
    pallas_call x1, Pallas kernels: 22.5 us -> 13.6 us  [sweep(): pl.pallas_call(sweep_kernel, grid=(channels // 2,), out_shape=[jax.ShapeD...]
    slice x6 -> x0, local copies, waits for them, and re-layouts: 3.94 us -> none  [the longest x1 1.08 us: on_device(): elevation[:, j]]
    unnamed x30 -> x20, local copies, waits for them, and re-layouts: 7.46 us -> 5.65 us
where the time goes in v1:
time: 90.2 us; the launch traced here: 88.5 us
  Pallas kernels  70.1 us (78%)
  local copies, waits for them, and re-layouts  9.95 us (11%)
  other arithmetic  4.69 us (5%)
  matrix products  2.85 us (3%)
    pallas_call x1, Pallas kernels, transform(): pl.pallas_call(functools.partial(transform_kernel, factors, lon_size, gro...  56.6 us
    pallas_call x1, Pallas kernels, sweep(): pl.pallas_call(sweep_kernel, grid=(channels // 2,), out_shape=[jax.ShapeD...  13.6 us
    unnamed x20, local copies, waits for them, and re-layouts  5.65 us
    dot_general x1, matrix products, on_device(): lax.dot_general(basis[:, :lon_cols], flat_field, (((1,), (1,)), ((), ()))...  2.85 us

profile of v1, /device:TPU:13, one launch (start us, length us, event | category | flops | bytes accessed | tf_op | source)
XLA Modules:
  0.0 88.5 jit_solution(9391586506807111563)
XLA Ops:
  0.6 0.0 copy-start
  0.7 0.6 add_convert_fusion.pole_ref
  1.2 0.7 compare_select_fusion.5
  1.9 0.1 add_cosine_fusion
  2.0 0.1 broadcast_divide_fusion
  2.1 0.1 multiply_sine_fusion.2
  2.2 0.1 multiply_sine_fusion.1
  2.3 0.8 multiply_cosine_fusion
  3.1 0.1 copy.31.weight_ref
  3.2 0.1 copy.30.lat_ref
  3.3 0.9 %convert_element_type.67 = f32[64,512]{1,0:T(8,128)S(1)} convert(s32[64,512]{1,0:T(8,128)} %mask_ref.1) | non-fusion elementwise | flops 32768 | bytes 262144 | tf_op jit(solution)/shard_map/convert_element_type | solution.py:653
  4.2 1.1 %cosine_multiply_fusion = (f32[32,1,640]{2,0,1:T(8,128)S(1)}, f32[32,1,640]{2,0,1:T(8,128)S(1)}) fusion(f32[32]{0:T(128)S(1)} %compare_select_fusion.5, s32[640]{0:T(1024)S(1)} %add_select_fusion.1, s32[32]{0:T(128)} %param.14), kind=kLoop, calls=%fused_computation.14 | loop fusion | flops 327680 | bytes 166656 | tf_op jit(solution)/shard_map/mul | solution.py:31
  5.3 0.1 copy.25
  5.5 0.1 reshape.409.basis_ref
  5.6 1.4 %fusion.16 = (bf16[16,1,2048]{2,1,0:T(2,128)(2,1)S(1)}, bf16[16,1,2048]{2,1,0:T(2,128)(2,1)S(1)}) fusion(bf16[16,64,2048]{2,1,0:T(8,128)(2,1)} %leg_hbm.1), kind=kLoop, calls=%fused_computation.53 | loop fusion | bytes 262144 | tf_op jit(solution)/shard_map/slice | solution.py:679
  7.0 0.1 copy_bitcast_fusion
  7.1 0.0 copy-done
  7.1 0.3 broadcast_multiply_fusion
  7.4 0.0 copy-start.2
  7.4 0.0 copy-start.3
  7.4 0.0 copy-start.4
  7.4 2.8 %fusion = f32[64,1024]{1,0:T(8,128)} fusion(f32[1024,512]{1,0:T(8,128)S(1)} %bitcast.18, f32[64,640]{1,0:T(8,128)S(1)} %reshape.409.basis_ref), kind=kOutput, calls=%fused_computation.5 | convolution fusion | flops 402653184 | bytes 2490368 | tf_op jit(solution)/shard_map/dot_general | solution.py:681
  10.3 1.1 %reshape.411.part_ref = f32[2,16,32,64]{3,2,1,0:T(8,128)S(1)} reshape(f32[64,1024]{1,0:T(8,128)} %fusion) | data formatting | bytes 524288 | tf_op jit(solution)/shard_map/reshape | solution.py:688
  11.3 0.0 copy-done.2
  11.4 0.0 copy-done.3
  11.4 0.0 copy-done.4
  11.4 0.0 copy-start.1
  11.4 2.2 %copy-done.1 = bf16[16,64,2048]{2,1,0:T(8,128)(2,1)S(1)} copy-done((bf16[16,64,2048]{2,1,0:T(8,128)(2,1)S(1)}, bf16[16,64,2048]{2,1,0:T(8,128)(2,1)}, u32[]{:S(2)}) %copy-start.1) | copy-done | bytes 4194328
  13.6 0.0 copy-start.6
  13.6 0.7 copy-done.6
  14.3 56.6 %shard_map.121 = (f32[32,32,128]{2,1,0:T(8,128)S(1)}, f32[2,18,512]{2,1,0:T(8,128)S(1)}, f32[2,64,128]{2,1,0:T(8,128)S(1)}) custom-call(f32[2,16,32,64]{3,2,1,0:T(8,128)S(1)} %reshape.411.part_ref, bf16[16,64,2048]{2,1,0:T(8,128)(2,1)S(1)} %copy-done.1, f32[1,2048]{1,0:T(1,128)S(1)} %bitcast.17, bf16[2,16,2048]{2,1,0:T(8,128)(2,1)S(1)} %pad_maximum_fusion.1.leg_edges_ref, ...), custom_call_target="tpu_custom_call" | custom-call | flops 268435456 | bytes 4194304 | tf_op jit(solution)/shard_map/pallas_call | solution.py:589
  70.9 0.0 copy-start.5
  70.9 0.8 copy-done.5
  71.7 1.3 %copy.29.synth_ref = f32[16,72,64]{2,1,0:T(8,128)S(1)} copy(f32[16,72,64]{1,0,2:T(8,128)} %bitcast.16) | data formatting | bytes 589824 | tf_op jit(solution)/shard_map/reshape | solution.py:699
  72.9 0.0 copy-start.7
  73.0 0.6 copy-done.7
  73.6 0.0 copy-start.8
  73.6 0.7 copy-done.8
  74.3 0.0 copy-start.9
  74.3 0.7 copy-done.9
  74.9 13.6 %shard_map.122 = (f32[16,64,512]{2,1,0:T(8,128)}, f32[16,64,512]{2,1,0:T(8,128)}, f32[64,512]{1,0:T(8,128)}) custom-call(f32[8]{0:T(128)S(1)} %copy-done.7, f32[8]{0:T(128)S(1)} %copy-done.8, f32[2]{0:T(128)S(1)} %copy-done.9, f32[16,64,512]{2,1,0:T(8,128)S(1)} %copy-done, f32[64,512]{1,0:T(8,128)S(1)} %copy-done.3, f32[64,512]{1,0:T(8,128)S(1)} %copy-done.4, ...), custom_call_target="tpu_custom_call" | custom-call | tf_op jit(solution)/shard_map/pallas_call | solution.py:188
  (8 shorter events, 0.1 us)
Async XLA Ops:
  0.6 6.5 %copy-start = (f32[16,64,512]{2,1,0:T(8,128)S(1)}, f32[16,64,512]{2,1,0:T(8,128)}, u32[]{:S(2)}) copy-start(f32[16,64,512]{2,1,0:T(8,128)} %elev_ref.1) | copy-start | bytes 6291460
  7.4 4.0 %copy-start.2 = (s32[64,512]{1,0:T(8,128)S(1)}, s32[64,512]{1,0:T(8,128)}, u32[]{:S(2)}) copy-start(s32[64,512]{1,0:T(8,128)} %mask_ref.1) | copy-start | bytes 393220
  7.4 4.0 %copy-start.3 = (f32[64,512]{1,0:T(8,128)S(1)}, f32[64,512]{1,0:T(8,128)}, u32[]{:S(2)}) copy-start(f32[64,512]{1,0:T(8,128)} %depth_ref.1) | copy-start | bytes 393220
  7.4 4.0 %copy-start.4 = (f32[64,512]{1,0:T(8,128)S(1)}, f32[64,512]{1,0:T(8,128)}, u32[]{:S(2)}) copy-start(f32[64,512]{1,0:T(8,128)} %drag_ref.1) | copy-start | bytes 393220
  11.4 2.2 %copy-start.1 = (bf16[16,64,2048]{2,1,0:T(8,128)(2,1)S(1)}, bf16[16,64,2048]{2,1,0:T(8,128)(2,1)}, u32[]{:S(2)}) copy-start(bf16[16,64,2048]{2,1,0:T(8,128)(2,1)} %leg_hbm.1) | copy-start | bytes 12582916
  13.6 0.7 copy-start.6
  70.9 0.8 copy-start.5
  72.9 0.7 copy-start.7
  73.6 0.7 copy-start.8
  74.3 0.7 copy-start.9

commit v2 on v1

--- a/solution.py
+++ b/solution.py
@@ -209,7 +209,7 @@
             pltpu.VMEM((lat_rows, channels, lon_cols), jnp.float32),
         ],
         compiler_params=pltpu.CompilerParams(
-            dimension_semantics=("arbitrary",), vmem_limit_bytes=40 * 1024 * 1024
+            dimension_semantics=("arbitrary",), vmem_limit_bytes=60 * 1024 * 1024
         ),
     )(
         jnp.asarray(FREQUENCIES, dtype=jnp.float32),
@@ -514,7 +514,7 @@
             synthesise(g)
 
     for wave in range(groups + 2 * phases):
-        for g in range(groups):
+        for g in reversed(range(groups)):
             stage = wave - g
             if stage == 0:
                 analyse(g)
@@ -630,7 +630,7 @@
             dma((6,)),
         ],
         compiler_params=pltpu.CompilerParams(
-            collective_id=0, has_side_effects=True, vmem_limit_bytes=40 * 1024 * 1024
+            collective_id=0, has_side_effects=True, vmem_limit_bytes=60 * 1024 * 1024
         ),
         cost_estimate=pl.CostEstimate(
             flops=4 * rows * lat_rows * degrees,

time: 90.2 us -> 85.9 us (0.952)
  local copies, waits for them, and re-layouts: 9.95 us -> 6.25 us
  other arithmetic: 4.69 us -> 5.94 us
    unnamed x20 -> x4, local copies, waits for them, and re-layouts: 5.65 us -> 0.01 us
    pallas_call x1, Pallas kernels: 56.6 us -> 54.4 us  [transform(): pl.pallas_call(functools.partial(transform_kernel, factors, lon_size, gro...]
    pallas_call x1, Pallas kernels: 13.6 us -> 14.7 us  [sweep(): pl.pallas_call(sweep_kernel, grid=(channels // 2,), out_shape=[jax.ShapeD...]
where the time goes in v2:
time: 85.9 us; the launch traced here: 84.3 us
  Pallas kernels  69.2 us (81%)
  local copies, waits for them, and re-layouts  6.25 us (7%)
  other arithmetic  5.94 us (7%)
  matrix products  2.14 us (2%)
    pallas_call x1, Pallas kernels, transform(): pl.pallas_call(functools.partial(transform_kernel, factors, lon_size, gro...  54.4 us
    pallas_call x1, Pallas kernels, sweep(): pl.pallas_call(sweep_kernel, grid=(channels // 2,), out_shape=[jax.ShapeD...  14.7 us
    dot_general x1, matrix products, on_device(): lax.dot_general(basis[:, :lon_cols], flat_field, (((1,), (1,)), ((), ()))...  2.14 us
    reshape x1, local copies, waits for them, and re-layouts, on_device(): synth.transpose(2, 3, 0, 1).reshape(channels, lat_rows + 8, basis.shape[0])  2.1 us

profile of v2, /device:TPU:13, one launch (start us, length us, event | category | flops | bytes accessed | tf_op | source)
XLA Modules:
  0.0 84.3 jit_solution(876620911253334815)
XLA Ops:
  0.6 0.0 copy-start
  0.7 0.7 add_convert_fusion.pole_ref
  1.3 0.7 compare_select_fusion.5
  2.0 0.1 add_cosine_fusion
  2.0 0.1 broadcast_divide_fusion
  2.1 0.1 multiply_sine_fusion.2
  2.2 0.1 multiply_sine_fusion.1
  2.3 0.6 pad_maximum_fusion.2.wave_ref
  3.0 0.8 multiply_cosine_fusion
  3.7 0.7 copy.31.weight_ref
  4.4 0.7 copy.30.lat_ref
  5.1 0.9 %convert_element_type.67 = f32[64,512]{1,0:T(8,128)S(1)} convert(s32[64,512]{1,0:T(8,128)} %mask_ref.1) | non-fusion elementwise | flops 32768 | bytes 262144 | tf_op jit(solution)/shard_map/convert_element_type | solution.py:653
  6.0 1.1 %cosine_multiply_fusion = (f32[32,1,640]{2,0,1:T(8,128)S(1)}, f32[32,1,640]{2,0,1:T(8,128)S(1)}) fusion(f32[32]{0:T(128)S(1)} %compare_select_fusion.5, s32[640]{0:T(1024)S(1)} %add_select_fusion.1, s32[32]{0:T(128)} %param.14), kind=kLoop, calls=%fused_computation.14 | loop fusion | flops 327680 | bytes 166656 | tf_op jit(solution)/shard_map/mul | solution.py:31
  7.1 0.1 copy.25
  7.3 0.1 reshape.409.basis_ref
  7.4 0.0 copy-start.1
  7.4 1.5 %fusion.16 = (bf16[16,1,2048]{2,1,0:T(2,128)(2,1)S(1)}, bf16[16,1,2048]{2,1,0:T(2,128)(2,1)S(1)}) fusion(bf16[16,64,2048]{2,1,0:T(8,128)(2,1)} %leg_hbm.1), kind=kLoop, calls=%fused_computation.53 | loop fusion | bytes 262144 | tf_op jit(solution)/shard_map/slice | solution.py:679
  8.9 0.1 copy_bitcast_fusion
  9.0 0.7 pad_maximum_fusion.1.leg_edges_ref
  9.6 0.0 copy-done
  9.6 0.2 broadcast_multiply_fusion
  9.9 0.0 copy-done.1
  9.9 2.1 %fusion = f32[64,1024]{1,0:T(8,128)S(1)} fusion(f32[1024,512]{1,0:T(8,128)S(1)} %bitcast.16, f32[64,640]{1,0:T(8,128)S(1)} %reshape.409.basis_ref), kind=kOutput, calls=%fused_computation.5 | convolution fusion | flops 402653184 | bytes 2490368 | tf_op jit(solution)/shard_map/dot_general | solution.py:681
  12.0 0.9 %reshape.411.part_ref = f32[2,16,32,64]{3,2,1,0:T(8,128)} reshape(f32[64,1024]{1,0:T(8,128)S(1)} %fusion) | data formatting | bytes 524288 | tf_op jit(solution)/shard_map/reshape | solution.py:688
  13.0 54.4 %shard_map.121 = (f32[32,32,128]{2,1,0:T(8,128)}, f32[2,18,512]{2,1,0:T(8,128)}, f32[2,64,128]{2,1,0:T(8,128)}) custom-call(f32[2,16,32,64]{3,2,1,0:T(8,128)} %reshape.411.part_ref, bf16[16,64,2048]{2,1,0:T(8,128)(2,1)} %leg_hbm.1, f32[1,2048]{1,0:T(1,128)} %bitcast.19, bf16[2,16,2048]{2,1,0:T(8,128)(2,1)} %pad_maximum_fusion.1.leg_edges_ref, ...), custom_call_target="tpu_custom_call" | custom-call | flops 268435456 | bytes 4194304 | tf_op jit(solution)/shard_map/pallas_call | solution.py:589
  67.4 2.1 %copy.29.synth_ref = f32[16,72,64]{2,1,0:T(8,128)} copy(f32[16,72,64]{1,0,2:T(8,128)} %bitcast.17) | data formatting | bytes 589824 | tf_op jit(solution)/shard_map/reshape | solution.py:699
  69.5 14.7 %shard_map.122 = (f32[16,64,512]{2,1,0:T(8,128)}, f32[16,64,512]{2,1,0:T(8,128)}, f32[64,512]{1,0:T(8,128)}) custom-call(f32[8]{0:T(128)} %constant.72.clone.omega_ref, f32[8]{0:T(128)} %constant.73.clone.amp_ref, f32[2]{0:T(128)} %add_convert_fusion.pole_ref, f32[16,64,512]{2,1,0:T(8,128)} %elev_ref.1, f32[64,512]{1,0:T(8,128)} %depth_ref.1, ...), custom_call_target="tpu_custom_call" | custom-call | tf_op jit(solution)/shard_map/pallas_call | solution.py:188
  (6 shorter events, 0.1 us)
Async XLA Ops:
  0.6 9.0 %copy-start = (f32[16,64,512]{2,1,0:T(8,128)S(1)}, f32[16,64,512]{2,1,0:T(8,128)}, u32[]{:S(2)}) copy-start(f32[16,64,512]{2,1,0:T(8,128)} %elev_ref.1) | copy-start | bytes 6291460
  7.4 2.5 %copy-start.1 = (f32[64,640]{1,0:T(8,128)}, f32[64,640]{1,0:T(8,128)S(1)}, u32[]{:S(2)}) copy-start(f32[64,640]{1,0:T(8,128)S(1)} %reshape.409.basis_ref) | copy-start | bytes 491524
